TPU v7x, 32 devices: a whole 2x2x4 slice. The times are simulated.
32 devices in a mesh: groups: 2 (over x), req: 8 (over z, core), row: 2 (over y).
Axes of the slice: x: 2, y: 2, z: 4, core: 2. Of those that a mesh axis runs over, the one named last changes fastest.
Arguments:
- latents: bfloat16 [16, 2, 4, 2560], P('groups', None, 'row', 'req'), parts along dimension 0, may hold values from -8 to 8
- dispatch_plan: int32 [16], P('groups'), parts along dimension 0, may hold values from 0 to 7, each once
- span_counts: int32 [8], P('groups'), parts along dimension 0, may hold values from 1 to 4, 8 in all
- in_weight: bfloat16 [432, 384], replicated, may hold values from -0.3125 to 0.3125
- in_bias: float32 [384], replicated, may hold values from -3 to 3
- norm_gain: float32 [384], replicated, may hold values from 0.5 to 1.5
- norm_bias: float32 [384], replicated, may hold values from -3 to 3
- mid_weight: bfloat16 [27, 384, 384], replicated, may hold values from -0.0625 to 0.0625
- mid_bias: float32 [384], replicated, may hold values from -3 to 3
Outputs:
- decoded: bfloat16 [16, 2, 4, 61440], P(('groups', 'req'), None, 'row'), parts along dimension 0
There are 2 independent parts, one for each index of `groups`. A program takes and returns all parts, laid end to end along the dimension named above; an argument that names none is the same for every part. Nothing has to cross between parts.
Inputs may be any that keep to these rules, and one draw needn't show every extreme that they name: `span_counts`: the counts sum to 8.
All inputs are finite; a program needn't handle non-finite values.
Results may differ from a plain program's by a relative error of at most 0.0029.
Values may be sent and summed in bfloat16 or wider, within the bound.
A program may use at most 64 MiB of HBM per device.

v0:
```python
import jax
import jax.numpy as jnp
from jax import lax
from jax.sharding import PartitionSpec as P

C_LAT = 16
G = 32
CF = 2
W = 160


def padded_2(cells, sides, width):
    for axis, dim in sides:
        count = lax.axis_size(axis)
        ends = count - 1
        head = lax.slice_in_dim(cells, 0, width, axis=dim)
        tail = lax.slice_in_dim(cells, cells.shape[dim] - width, cells.shape[dim], axis=dim)
        cells = jnp.concatenate(
            [
                lax.ppermute(tail, axis, [(i, (i + 1) % count) for i in range(ends)]),
                cells,
                lax.ppermute(head, axis, [((i + 1) % count, i) for i in range(ends)]),
            ],
            axis=dim,
        )
    return cells


def passed_along(block, axis, distance):
    devices = range(lax.axis_size(axis))
    route = [(i - distance, i) for i in devices if i - distance in devices]
    return lax.ppermute(block, axis, route)


def conv_input(frames, in_weight):
    frame_total, row_total, col_total, chans = frames.shape
    padded = jnp.pad(frames, ((0, 0), (0, 0), (1, 1), (0, 0)))
    out_frames = frame_total - 2
    out_rows = row_total - 2
    tap_list = []
    for time_off in range(3):
        for row_off in range(3):
            for col_off in range(3):
                tap_list.append(
                    padded[
                        time_off : time_off + out_frames,
                        row_off : row_off + out_rows,
                        col_off : col_off + col_total,
                        :,
                    ]
                )
    stacked = jnp.concatenate(tap_list, axis=-1).reshape(-1, 27 * chans)
    result = jnp.dot(stacked, in_weight, preferred_element_type=jnp.float32)
    return result.reshape(out_frames, out_rows, col_total, in_weight.shape[1])


def conv_hidden(frames, mid_weight):
    frame_total, row_total, col_total, chans = frames.shape
    padded = jnp.pad(frames, ((0, 0), (0, 0), (1, 1), (0, 0)))
    out_frames = frame_total - 2
    out_rows = row_total - 2
    running = jnp.zeros((out_frames * out_rows * col_total, mid_weight.shape[2]), jnp.float32)
    for time_off in range(3):
        for row_off in range(3):
            for col_off in range(3):
                tap_rows = padded[
                    time_off : time_off + out_frames,
                    row_off : row_off + out_rows,
                    col_off : col_off + col_total,
                    :,
                ].reshape(-1, chans)
                running = running + jnp.dot(
                    tap_rows,
                    mid_weight[(time_off * 3 + row_off) * 3 + col_off],
                    preferred_element_type=jnp.float32,
                )
    return running.reshape(out_frames, out_rows, col_total, mid_weight.shape[2])


def group_stats(hidden, groups):
    frame_total = hidden.shape[0]
    grouped = hidden.reshape(frame_total, -1, groups, hidden.shape[3] // groups)
    return (jnp.sum(grouped, axis=(1, 3)), jnp.sum(grouped * grouped, axis=(1, 3)))


def normalize(hidden, group_sums, squares, cell_count, norm_gain, norm_bias, groups):
    per_group = hidden.shape[3] // groups
    mean_val = group_sums / cell_count
    var_val = squares / cell_count - mean_val * mean_val
    inverse = lax.rsqrt(var_val + 1e-06)
    mean_chan = jnp.repeat(mean_val, per_group, axis=-1)[:, None, None, :]
    inv_chan = jnp.repeat(inverse, per_group, axis=-1)[:, None, None, :]
    normed = (hidden - mean_chan) * inv_chan * norm_gain + norm_bias
    return jax.nn.silu(normed).astype(jnp.bfloat16)


def local(
    latents,
    dispatch_plan,
    span_counts,
    in_weight,
    in_bias,
    norm_gain,
    norm_bias,
    mid_weight,
    mid_bias,
):
    req_count = lax.axis_size("req")
    row_count = lax.axis_size("row")
    my_index = lax.axis_index("req")
    rows_here = latents.shape[2]
    channels = mid_weight.shape[2]
    starts = jnp.cumsum(span_counts) - span_counts
    span_depth = 2
    halo_depth = 2
    offsets = jnp.arange(span_depth, dtype=jnp.int32) - (span_depth - 1)
    wanted = jnp.arange(req_count, dtype=jnp.int32)[:, None] + offsets[None, :]
    chosen = jnp.take(dispatch_plan, jnp.maximum(wanted, 0).reshape(-1), axis=0)
    selected = jnp.take(latents, chosen, axis=0)
    arrived = lax.all_to_all(selected, "req", split_axis=0, concat_axis=3, tiled=True)
    source = my_index + offsets
    broken = jnp.any((starts[None, :] > source[:, None]) & (starts[None, :] <= my_index), axis=1)
    valid_mask = jnp.where(broken, 0.0, 1.0).astype(jnp.bfloat16)
    arrived = arrived * valid_mask[:, None, None, None]
    frames = arrived.reshape(span_depth * CF, rows_here, W * C_LAT)
    frames = padded_2(frames, (("row", 1),), halo_depth)
    frames = frames.reshape(span_depth * CF, rows_here + 2 * halo_depth, W, C_LAT)
    hidden_all = conv_input(frames, in_weight) + in_bias
    hidden = hidden_all[:, 1 : rows_here + 1]
    group_sums, squares = group_stats(hidden, G)
    group_sums, squares = lax.psum((group_sums, squares), "row")
    cell_count = row_count * rows_here * W * (channels // G)
    active = normalize(hidden_all, group_sums, squares, cell_count, norm_gain, norm_bias, G)
    out_frames = active.shape[0]
    row_place = lax.axis_index("row") * rows_here + jnp.arange(rows_here + 2, dtype=jnp.int32) - 1
    inside = jnp.where((row_place >= 0) & (row_place < row_count * rows_here), 1.0, 0.0).astype(
        jnp.bfloat16
    )
    active = active * inside[None, :, None, None]
    active = active.reshape(out_frames, active.shape[1], W * channels)
    keep_prev = valid_mask[span_depth - 2]
    cache_frames = passed_along(active, "req", 1) * keep_prev
    conv_frames = jnp.concatenate([cache_frames, active], axis=0)
    conv_frames = conv_frames.reshape(2 * CF, rows_here + 2, W, channels)
    mixed = conv_hidden(conv_frames, mid_weight) + mid_bias + hidden
    return mixed.astype(jnp.bfloat16).reshape(1, CF, rows_here, W * channels)


def solution(mesh):
    placed = (
        P("groups", None, "row", "req"),
        P("groups"),
        P("groups"),
        P(),
        P(),
        P(),
        P(),
        P(),
        P(),
    )
    return jax.shard_map(
        local,
        mesh=mesh,
        in_specs=placed,
        out_specs=P(("groups", "req"), None, "row", None),
        check_vma=False,
    )
```

profile of v0, /device:TPU:14, one launch (start us, length us, event | category | flops | bytes accessed | tf_op | source)
XLA Modules:
  0.0 81.9 jit_solution(8413687064218551289)
XLA Ops:
  0.3 1.3 %gather_fusion = s32[16]{0:T(128)S(1)} fusion(s32[8]{0:T(128)} %param.10, s32[1024]{0:T(1024)S(1)} %pad_clamp_fusion.1), kind=kCustom, calls=%fused_computation | custom fusion | bytes 192 | tf_op jit(solution)/shard_map/jit(_take)/gather | solution.py:118
  1.7 1.4 %gather_fusion.1 = bf16[16,2,2,320]{3,2,1,0:T(2,128)(2,1)S(1)} fusion(bf16[8,2,2,320]{3,2,1,0:T(2,128)(2,1)} %param.9, s32[1024]{0:T(1024)S(1)} %pad_clamp_fusion), kind=kCustom, calls=%fused_computation.1 | custom fusion | bytes 81984 | tf_op jit(solution)/shard_map/jit(_take)/gather | solution.py:119
  3.1 0.7 broadcast_select_fusion
  3.8 5.3 %all-to-all-start = ((bf16[16,2,2,320]{3,2,1,0:T(2,128)(2,1)}), bf16[16,2,2,320]{3,2,1,0:T(2,128)(2,1)S(1)}, u32[]{:S(2)}, u32[]{:S(2)}) async-start(bf16[16,2,2,320]{3,2,1,0:T(2,128)(2,1)} %broadcast_select_fusion), calls=%async_computation | async-start | bytes 98304 | tf_op jit(solution)/shard_map/all_to_all | solution.py:120
  9.1 0.8 %reduce-window.9 = s32[4,1]{0,1:T(1,128)S(1)} reduce-window(s32[4,1]{0,1:T(1,128)} %bitcast.204, s32[]{:T(128)} %constant.58.clone.1), window={size=4x1 pad=3_0x0_0}, to_apply=%region_0.0 | reduce-window | flops 12 | bytes 36 | tf_op jit(solution)/shard_map/reduce-window.4
  10.0 0.7 broadcast_compare_fusion.1
  10.6 0.2 and_reduce_fusion
  11.0 2.6 %all-to-all-done = bf16[16,2,2,320]{3,2,1,0:T(2,128)(2,1)S(1)} async-done(((bf16[16,2,2,320]{3,2,1,0:T(2,128)(2,1)}), bf16[16,2,2,320]{3,2,1,0:T(2,128)(2,1)S(1)}, u32[]{:S(2)}, u32[]{:S(2)}) %all-to-all-start) | async-done | bytes 40992 | tf_op jit(solution)/shard_map/all_to_all | solution.py:120
  13.6 0.1 all_to_all.18
  13.9 2.4 %collective-permute-start.1 = (bf16[4,2,2560]{2,1,0:T(2,128)(2,1)S(1)}, bf16[4,2,2560]{2,1,0:T(2,128)(2,1)S(1)}, u32[]{:S(2)}, u32[]{:S(2)}) collective-permute-start(bf16[4,2,2560]{2,1,0:T(2,128)(2,1)S(1)} %broadcast_multiply_fusion.2), channel_id=1, source_target_pairs={{1,0},{3,2},{5,4},{7,6},{9,8},{11,10},{13,12},{15,14},{17,16},{19,... | collective-permute-start | bytes 122888 | tf_op jit(solution)/shard_map/ppermute | solution.py:22
  16.3 1.3 %collective-permute-start = (bf16[4,2,2560]{2,1,0:T(2,128)(2,1)S(1)}, bf16[4,2,2560]{2,1,0:T(2,128)(2,1)S(1)}, u32[]{:S(2)}, u32[]{:S(2)}) collective-permute-start(bf16[4,2,2560]{2,1,0:T(2,128)(2,1)S(1)} %broadcast_multiply_fusion.2), channel_id=1, source_target_pairs={{0,1},{2,3},{4,5},{6,7},{8,9},{10,11},{12,13},{14,15},{16,17},{18,... | collective-permute-start | bytes 122888 | tf_op jit(solution)/shard_map/ppermute | solution.py:20
  17.6 0.2 all_to_all.19
  17.9 4.2 %collective-permute-done = bf16[4,2,2560]{2,1,0:T(2,128)(2,1)S(1)} collective-permute-done((bf16[4,2,2560]{2,1,0:T(2,128)(2,1)S(1)}, bf16[4,2,2560]{2,1,0:T(2,128)(2,1)S(1)}, u32[]{:S(2)}, u32[]{:S(2)}) %collective-permute-start) | collective-permute-done | bytes 40992 | tf_op jit(solution)/shard_map/ppermute | solution.py:20
  22.2 0.3 concatenate.27
  22.5 0.3 concatenate.28
  22.7 0.2 pad_maximum_fusion.1
  23.0 1.2 %pad_maximum_fusion.2 = (bf16[2,4,160,16]{3,2,1,0:T(8,128)(2,1)S(1)}, bf16[2,4,160,16]{3,2,1,0:T(8,128)(2,1)S(1)}, bf16[2,4,160,16]{3,2,1,0:T(8,128)(2,1)S(1)}, ...) fusion(bf16[4,2,160,16]{3,2,1,0:T(8,128)(2,1)S(1)} %concatenate, ...), kind=kLoop, calls=%fused_computation.59 | loop fusion | flops 491520 | bytes 532480 | tf_op jit(solution)/shard_map/concatenate | solution.py:18
  24.1 1.9 %pad_slice_fusion.14 = (bf16[2,4,160,16]{3,2,1,0:T(8,128)(2,1)S(1)}, bf16[2,4,160,16]{3,2,1,0:T(8,128)(2,1)S(1)}, bf16[2,4,160,16]{3,2,1,0:T(8,128)(2,1)}, bf16[...) fusion(bf16[4,6,160,16]{3,2,1,0:T(8,128)(2,1)S(1)} %pad_maximum, ...), kind=kLoop, calls=%fused_computation.139 | loop fusion | bytes 1720320 | tf_op jit(solution)/shard_map/slice | solution.py:45
  26.0 1.9 %pad_slice_fusion.15 = (bf16[2,4,160,16]{3,2,1,0:T(8,128)(2,1)}, bf16[2,4,160,16]{3,2,1,0:T(8,128)(2,1)}, bf16[2,4,160,16]{3,2,1,0:T(8,128)(2,1)}, bf16[2,4,160,...) fusion(bf16[4,6,160,16]{3,2,1,0:T(8,128)(2,1)S(1)} %pad_maximum, ...), kind=kLoop, calls=%fused_computation.140 | loop fusion | bytes 2048000 | tf_op jit(solution)/shard_map/slice | solution.py:45
  28.0 8.2 %concatenate.32 = bf16[2,4,160,432]{3,2,1,0:T(8,128)(2,1)} concatenate(bf16[2,4,160,16]{3,2,1,0:T(8,128)(2,1)S(1)} %copy-done.4, bf16[2,4,160,16]{3,2,1,0:T(8,128)(2,1)S(1)} %get-tuple-element.65, bf16[2,4,160,16]{3,2,1,0:T(8,128)(2,1)S(1)} %get-tuple-element.39, bf16[2,4,160,16]{3,2,1,0:T(8,128)(2,1)} %get-tuple-element.40, bf16[2,4,160,16]{3,2,1,0:T(8,128)(2,1)} %get-tuple-element.57, ...), dimensions={3} | concatenate | bytes 2211840 | tf_op jit(solution)/shard_map/concatenate | solution.py:52
  36.2 2.2 %convolution_add_fusion = f32[2,4,160,384]{3,2,1,0:T(8,128)S(1)} fusion(bf16[2,4,160,432]{3,2,1,0:T(8,128)(2,1)} %concatenate.32, f32[384]{0:T(512)S(1)} %copy-done.8, bf16[432,384]{1,0:T(8,128)(2,1)S(1)} %copy-done), kind=kOutput, calls=%fused_computation.10 | convolution fusion | flops 425164800 | bytes 3405312 | tf_op jit(solution)/shard_map/dot_general | solution.py:53
  38.4 0.1 slice_reduce_fusion
  39.0 4.9 %all-reduce.2 = (f32[2,32]{1,0:T(2,128)S(1)}, f32[2,32]{1,0:T(2,128)S(1)}) all-reduce(f32[2,32]{1,0:T(2,128)S(1)} %reduce_sum.37, f32[2,32]{1,0:T(2,128)S(1)} %reduce_sum.25), channel_id=1, replica_groups=mesh['groups'=2,'req'=8,'row'=2] {'row'}, use_global_device_ids=true, to_apply=%region_7.8 | all-reduce | flops 128 | bytes 1024 | tf_op jit(solution)/shard_map/psum | solution.py:131
  44.0 0.1 sub.30
  44.3 0.7 fusion
  45.0 1.2 %reshape.244 = bf16[2,4,61440]{2,1,0:T(4,128)(2,1)} reshape(bf16[2,4,160,384]{3,2,1,0:T(8,128)(2,1)S(1)} %fusion) | data formatting | bytes 1966080 | tf_op jit(solution)/shard_map/reshape | solution.py:140
  46.2 1.9 %collective-permute-start.2 = (bf16[2,4,61440]{2,1,0:T(4,128)(2,1)}, bf16[2,4,61440]{2,1,0:T(4,128)(2,1)S(1)}, u32[]{:S(2)}, u32[]{:S(2)}) collective-permute-start(bf16[2,4,61440]{2,1,0:T(4,128)(2,1)} %reshape.244), channel_id=1, source_target_pairs={{0,2},{2,4},{4,6},{6,8},{8,10},{10,12},{12,14},{1,3},{3,5},{5,7},{... | collective-permute-start | bytes 2949128 | tf_op jit(solution)/shard_map/ppermute | solution.py:32
  48.1 13.7 %collective-permute-done.2 = bf16[2,4,61440]{2,1,0:T(4,128)(2,1)S(1)} collective-permute-done((bf16[2,4,61440]{2,1,0:T(4,128)(2,1)}, bf16[2,4,61440]{2,1,0:T(4,128)(2,1)S(1)}, u32[]{:S(2)}, u32[]{:S(2)}) %collective-permute-start.2) | collective-permute-done | bytes 983072 | tf_op jit(solution)/shard_map/ppermute | solution.py:32
  61.8 1.1 %broadcast_multiply_fusion = bf16[1,8,61440]{2,1,0:T(8,128)(2,1)} fusion(bf16[1,8,61440]{2,1,0:T(8,128)(2,1)S(1)} %bitcast.199, bf16[]{:T(256)S(1)} %bitcast.203), kind=kLoop, calls=%fused_computation.53 | loop fusion | flops 491520 | bytes 1966082 | tf_op jit(solution)/shard_map/mul | solution.py:142
  62.9 1.9 %concatenate.33 = bf16[2,4,160,384]{3,2,1,0:T(8,128)(2,1)S(1)} reshape(bf16[2,4,61440]{2,1,0:T(4,128)(2,1)} %bitcast.170) | data formatting | bytes 1966080 | tf_op jit(solution)/shard_map/concatenate | solution.py:143
  64.7 0.2 pad_maximum_fusion
  65.0 0.5 fusion.3
  65.5 0.9 %pad_slice_fusion.32 = (bf16[2,2,160,384]{3,2,1,0:T(8,128)(2,1)S(1)}, bf16[2,2,160,384]{3,2,1,0:T(8,128)(2,1)S(1)}, bf16[2,2,160,384]{3,2,1,0:T(8,128)(2,1)S(1)}...) fusion(bf16[4,4,160,384]{3,2,1,0:T(8,128)(2,1)S(1)} %pad_maximu, ...), kind=kLoop, calls=%fused_computation.157 | loop fusion | bytes 6389760 | tf_op jit(solution)/shard_map/slice | solution.py:66
  66.3 0.8 %pad_slice_fusion.33 = (bf16[2,2,160,384]{3,2,1,0:T(8,128)(2,1)S(1)}, bf16[2,2,160,384]{3,2,1,0:T(8,128)(2,1)S(1)}, bf16[2,2,160,384]{3,2,1,0:T(8,128)(2,1)S(1)}...) fusion(bf16[4,4,160,384]{3,2,1,0:T(8,128)(2,1)S(1)} %pad_maximu, ...), kind=kLoop, calls=%fused_computation.158 | loop fusion | bytes 6389760 | tf_op jit(solution)/shard_map/slice | solution.py:66
  67.2 1.3 %slice-done.1 = s8[3768320]{0:T(1024)(128)(4,1)S(1)} async-done(((s8[7962624]{0:T(1024)(128)(4,1)}), s8[3768320]{0:T(1024)(128)(4,1)S(1)}, s32[]{:S(2)}) %slice-start.1) | async-done | bytes 3768344
  68.4 0.4 fusion.35
  68.9 0.5 convolution_add_fusion.26
  69.4 0.4 convolution_add_fusion.25
  69.8 0.5 convolution_add_fusion.24
  70.3 0.4 convolution_add_fusion.23
  70.7 0.4 convolution_add_fusion.22
  71.2 0.5 convolution_add_fusion.21
  71.7 0.4 convolution_add_fusion.20
  72.1 0.5 convolution_add_fusion.19
  72.6 0.4 convolution_add_fusion.18
  73.0 0.4 convolution_add_fusion.17
  73.5 0.5 convolution_add_fusion.16
  73.9 0.4 convolution_add_fusion.15
  74.4 0.5 convolution_add_fusion.14
  74.9 0.4 convolution_add_fusion.13
  75.3 0.4 convolution_add_fusion.12
  75.8 0.5 convolution_add_fusion.11
  76.2 0.4 convolution_add_fusion.10
  76.7 0.5 convolution_add_fusion.9
  77.1 0.4 convolution_add_fusion.8
  77.6 0.4 convolution_add_fusion.7
  78.1 0.4 convolution_add_fusion.6
  78.6 0.4 convolution_add_fusion.5
  79.0 0.4 convolution_add_fusion.4
  79.5 0.5 convolution_add_fusion.3
  79.9 0.4 convolution_add_fusion.2
  80.4 0.5 convolution_add_fusion.1
  80.9 0.1 add_convert_fusion
  81.0 0.9 %reshape.273 = bf16[1,2,2,61440]{3,2,1,0:T(2,128)(2,1)} reshape(bf16[2,2,160,384]{3,2,1,0:T(8,128)(2,1)S(1)} %add_convert_fusion) | data formatting | bytes 983040 | tf_op jit(solution)/shard_map/reshape | solution.py:146
  (49 shorter events, 1.4 us)
Async XLA Ops:
  0.0 36.2 %copy-start = (bf16[432,384]{1,0:T(8,128)(2,1)S(1)}, bf16[432,384]{1,0:T(8,128)(2,1)}, u32[]{:S(2)}) copy-start(bf16[432,384]{1,0:T(8,128)(2,1)} %param.12) | copy-start | bytes 995332
  3.8 9.8 %all-to-all-start = ((bf16[16,2,2,320]{3,2,1,0:T(2,128)(2,1)}), bf16[16,2,2,320]{3,2,1,0:T(2,128)(2,1)S(1)}, u32[]{:S(2)}, u32[]{:S(2)}) async-start(bf16[16,2,2,320]{3,2,1,0:T(2,128)(2,1)} %broadcast_select_fusion), calls=%async_computation | async-start | bytes 98304 | tf_op jit(solution)/shard_map/all_to_all | solution.py:120
  13.9 8.6 %collective-permute-start.1 = (bf16[4,2,2560]{2,1,0:T(2,128)(2,1)S(1)}, bf16[4,2,2560]{2,1,0:T(2,128)(2,1)S(1)}, u32[]{:S(2)}, u32[]{:S(2)}) collective-permute-start(bf16[4,2,2560]{2,1,0:T(2,128)(2,1)S(1)} %broadcast_multiply_fusion.2), channel_id=1, source_target_pairs={{1,0},{3,2},{5,4},{7,6},{9,8},{11,10},{13,12},{15,14},{17,16},{19,... | collective-permute-start | bytes 122888 | tf_op jit(solution)/shard_map/ppermute | solution.py:22
  16.3 5.9 %collective-permute-start = (bf16[4,2,2560]{2,1,0:T(2,128)(2,1)S(1)}, bf16[4,2,2560]{2,1,0:T(2,128)(2,1)S(1)}, u32[]{:S(2)}, u32[]{:S(2)}) collective-permute-start(bf16[4,2,2560]{2,1,0:T(2,128)(2,1)S(1)} %broadcast_multiply_fusion.2), channel_id=1, source_target_pairs={{0,1},{2,3},{4,5},{6,7},{8,9},{10,11},{12,13},{14,15},{16,17},{18,... | collective-permute-start | bytes 122888 | tf_op jit(solution)/shard_map/ppermute | solution.py:20
  24.1 3.9 %copy-start.4 = (bf16[2,4,160,16]{3,2,1,0:T(8,128)(2,1)S(1)}, bf16[2,4,160,16]{3,2,1,0:T(8,128)(2,1)}, u32[]{:S(2)}) copy-start(bf16[2,4,160,16]{3,2,1,0:T(8,128)(2,1)} %get-tuple-element.69) | copy-start | bytes 122884
  26.0 10.2 %copy-start.8 = (f32[384]{0:T(512)S(1)}, f32[384]{0:T(512)}, u32[]{:S(2)}) copy-start(f32[384]{0:T(512)} %param.13) | copy-start | bytes 4612
  28.0 16.3 %copy-start.5 = (f32[384]{0:T(512)S(1)}, f32[384]{0:T(512)}, u32[]{:S(2)}) copy-start(f32[384]{0:T(512)} %param.15) | copy-start | bytes 4612
  28.0 16.3 %copy-start.6 = (f32[384]{0:T(512)S(1)}, f32[384]{0:T(512)}, u32[]{:S(2)}) copy-start(f32[384]{0:T(512)} %param.14) | copy-start | bytes 4612
  38.4 24.5 %copy-start.2 = (f32[2,4,160,384]{3,2,1,0:T(8,128)}, f32[2,4,160,384]{3,2,1,0:T(8,128)S(1)}, u32[]{:S(2)}) copy-start(f32[2,4,160,384]{3,2,1,0:T(8,128)S(1)} %convolution_add_fusion) | copy-start | bytes 5898244
  46.2 15.6 %collective-permute-start.2 = (bf16[2,4,61440]{2,1,0:T(4,128)(2,1)}, bf16[2,4,61440]{2,1,0:T(4,128)(2,1)S(1)}, u32[]{:S(2)}, u32[]{:S(2)}) collective-permute-start(bf16[2,4,61440]{2,1,0:T(4,128)(2,1)} %reshape.244), channel_id=1, source_target_pairs={{0,2},{2,4},{4,6},{6,8},{8,10},{10,12},{12,14},{1,3},{3,5},{5,7},{... | collective-permute-start | bytes 2949128 | tf_op jit(solution)/shard_map/ppermute | solution.py:32
  65.0 2.2 %slice-start = ((s8[7962624]{0:T(1024)(128)(4,1)}), s8[4194304]{0:T(1024)(128)(4,1)S(1)}, s32[]{:S(2)}) async-start(s8[7962624]{0:T(1024)(128)(4,1)} %bitcast.168), calls=%async_computation.1 | async-start | bytes 8388608
  65.5 3.0 %slice-start.1 = ((s8[7962624]{0:T(1024)(128)(4,1)}), s8[3768320]{0:T(1024)(128)(4,1)S(1)}, s32[]{:S(2)}) async-start(s8[7962624]{0:T(1024)(128)(4,1)} %bitcast.168), calls=%async_computation.2 | async-start | bytes 7536640
  78.1 2.8 %copy-start.3 = (f32[2,4,160,384]{3,2,1,0:T(8,128)S(1)}, f32[2,4,160,384]{3,2,1,0:T(8,128)}, u32[]{:S(2)}) copy-start(f32[2,4,160,384]{3,2,1,0:T(8,128)} %copy-done.2) | copy-start | bytes 5898244
  78.1 2.8 %copy-start.7 = (f32[384]{0:T(512)S(1)}, f32[384]{0:T(512)}, u32[]{:S(2)}) copy-start(f32[384]{0:T(512)} %param.17) | copy-start | bytes 4612
  78.5 3.3 %copy-start.1 = (bf16[432,384]{1,0:T(8,128)(2,1)S(1)}, bf16[432,384]{1,0:T(8,128)(2,1)}, u32[]{:S(2)}) copy-start(bf16[432,384]{1,0:T(8,128)(2,1)} %param.12) | copy-start | bytes 995332
where the time goes:
time: 83.1 us; the launch traced here: 81.9 us
  local copies, waits for them, and re-layouts  23.6 us (28%)
  waiting for transfers between devices  20.6 us (25%)
  matrix products  14.3 us (17%)
  starting transfers between devices  10.9 us (13%)
  other arithmetic  6.98 us (8%)
  blocking collectives  4.93 us (6%)
    ppermute x1, waiting for transfers between devices, passed_along(): return lax.ppermute(block, axis, route)  13.7 us
    dot_general x27, matrix products, conv_hidden(): jnp.dot(tap_rows, mid_weight[(time_off * 3 + row_off) * 3 + col_off], pre...  12.2 us
    concatenate x1, local copies, waits for them, and re-layouts, conv_input(): stacked = jnp.concatenate(tap_list, axis=-1).reshape(-1, 27 * chans)  8.21 us
    all_to_all x1, starting transfers between devices, local(): lax.all_to_all(selected, 'req', split_axis=0, concat_axis=3, tiled=True)  5.32 us
    psum x1, blocking collectives, local(): group_sums, squares = lax.psum((group_sums, squares), 'row')  4.93 us
    ppermute x1, waiting for transfers between devices, padded_2(): lax.ppermute(tail, axis, [(i, (i + 1) % count) for i in range(ends)])  4.24 us
    slice x2, local copies, waits for them, and re-layouts, conv_input(): padded[time_off:time_off + out_frames, row_off:row_off + out_rows, col_of...  3.84 us
    all_to_all x1, waiting for transfers between devices, local(): lax.all_to_all(selected, 'req', split_axis=0, concat_axis=3, tiled=True)  2.65 us
  transfers between devices with their start and end apart: 4, of which 3 were waited for; matrix products, arithmetic and copies ran while one was open for 3% of the time, Pallas kernels for 0%

commit v1 on v0

v1 whole, which is shorter than its diff:
```python
import functools

import jax
import jax.numpy as jnp
from jax import lax
from jax.experimental import pallas as pl
from jax.experimental.pallas import tpu as pltpu
from jax.sharding import PartitionSpec as P

C_LAT = 16
G = 32
CF = 2
W = 160
LANES = 128
DEPTH = 3
MESH = pl.DeviceIdType.MESH


def exchange_kernel(req_n, row_n, plan_ref, lat_ref, out_ref, sel, send_sems, recv_sems):
    me_req = lax.axis_index("req")
    me_row = lax.axis_index("row")
    total = req_n * row_n
    flat = me_row * req_n + me_req
    barrier = pltpu.get_barrier_semaphore()

    def place(k):
        target = lax.rem(flat + k, total)
        return {"row": target // req_n, "req": lax.rem(target, req_n)}

    for k in range(1, total):
        pl.semaphore_signal(barrier, inc=1, device_id=place(k), device_id_type=MESH)
    for d in range(DEPTH - 1):
        sel[d] = jnp.zeros_like(sel[d])
    for d in range(req_n):
        sel[d + DEPTH - 1] = lat_ref[plan_ref[d]]
    pl.semaphore_wait(barrier, total - 1)
    copies = []
    for k in range(1, total):
        where = place(k)
        copy = pltpu.make_async_remote_copy(
            src_ref=sel.at[pl.ds(where["req"], DEPTH)],
            dst_ref=out_ref.at[me_row, me_req],
            send_sem=send_sems.at[k],
            recv_sem=recv_sems.at[k],
            device_id=where,
            device_id_type=MESH,
        )
        copy.start()
        copies.append(copy)
    out_ref[me_row, me_req] = sel[pl.ds(me_req, DEPTH)]
    for copy in copies:
        copy.wait()


def exchange(latents, plan):
    req_n = lax.axis_size("req")
    row_n = lax.axis_size("row")
    slots, frames, rows, lanes = latents.shape
    return pl.pallas_call(
        functools.partial(exchange_kernel, req_n, row_n),
        out_shape=jax.ShapeDtypeStruct((row_n, req_n, DEPTH, frames, rows, lanes), latents.dtype),
        in_specs=[
            pl.BlockSpec(memory_space=pltpu.SMEM),
            pl.BlockSpec(memory_space=pltpu.VMEM),
        ],
        out_specs=pl.BlockSpec(memory_space=pltpu.VMEM),
        scratch_shapes=[
            pltpu.VMEM((req_n + DEPTH - 1, frames, rows, lanes), latents.dtype),
            pltpu.SemaphoreType.DMA((req_n * row_n,)),
            pltpu.SemaphoreType.DMA((req_n * row_n,)),
        ],
        compiler_params=pltpu.CompilerParams(collective_id=0, has_side_effects=True),
        name="span_exchange",
    )(plan, latents)


def decode_kernel(
    rows_here,
    counts_ref,
    x_ref,
    in_w_ref,
    in_b_ref,
    gain_ref,
    nbias_ref,
    mid_b_ref,
    mid_w_hbm,
    out_ref,
    mid_w,
    in_w,
    pair_rows,
    pair_time,
    hid,
    act,
    sems,
):
    frames_in, height, blocks, _ = x_ref.shape
    chans = in_w_ref.shape[1]
    outs = frames_in - 2
    width = blocks * (LANES // C_LAT)
    me = lax.axis_index("req")
    row0 = lax.axis_index("row") * rows_here

    copies = []
    for tap in range(9):
        copy = pltpu.make_async_copy(
            mid_w_hbm.at[pl.ds(3 * tap, 3)], mid_w.at[pl.ds(3 * tap, 3)], sems.at[tap]
        )
        copy.start()
        copies.append(copy)

    def keep_of(d):
        start = jnp.int32(0)
        first = d <= 0
        for r in range(counts_ref.shape[0]):
            first = jnp.logical_or(first, start == d)
            start = start + counts_ref[r]
        return jnp.where(first, 0.0, 1.0).astype(jnp.float32)

    keep_own = keep_of(me)
    keep_prev = keep_of(me - 1)

    half = LANES // 2
    three = 3 * C_LAT
    in_w[...] = jnp.zeros_like(in_w)
    for t in range(3):
        for i in range(3):
            if i < 2:
                base = t * LANES + i * half
            else:
                base = 3 * LANES + t * half
            in_w[base : base + three, :] = in_w_ref[(3 * t + i) * three : (3 * t + i + 1) * three, :]

    zero_slab = jnp.zeros((width, LANES), jnp.bfloat16)
    for f in range(frames_in):
        pair_rows[f, 0] = zero_slab
    for f in range(frames_in + 1):
        pair_time[f, height] = zero_slab
    for y in range(height):
        pair_time[frames_in, y] = zero_slab

    place = lax.broadcasted_iota(jnp.int32, (width, LANES), 0) % 8
    lane = lax.broadcasted_iota(jnp.int32, (width, LANES), 1)
    low = jnp.logical_and(place == 0, lane < C_LAT)
    high = jnp.logical_and(place == 7, jnp.logical_and(lane >= 2 * C_LAT, lane < three))
    bits = [lax.rem(place // (1 << n), 2) == 1 for n in range(3)]
    edge = jnp.zeros((8, LANES), jnp.float32)

    @pl.loop(0, frames_in)
    def _(f):
        keep = jnp.where(f < CF, keep_prev, jnp.where(f < 2 * CF, keep_own, 1.0))

        @pl.loop(0, height)
        def _(y):
            cells = x_ref[f, y].astype(jnp.float32) * keep
            spread = jnp.broadcast_to(cells[:, None, :], (blocks, 8, LANES)).reshape(width, LANES)
            turned = jnp.where(bits[0], spread, pltpu.roll(spread, C_LAT, 1))
            turned = jnp.where(bits[1], pltpu.roll(turned, LANES - 2 * C_LAT, 1), turned)
            turned = jnp.where(bits[2], pltpu.roll(turned, LANES - 4 * C_LAT, 1), turned)
            before = jnp.concatenate([edge, turned[:-8]], axis=0)
            after = jnp.concatenate([turned[8:], edge], axis=0)
            window = jnp.where(low, before, jnp.where(high, after, turned))
            other = pltpu.roll(window, half, 1).astype(jnp.bfloat16)
            window = window.astype(jnp.bfloat16)
            pair_rows[f, y + 1, :, :half] = window[:, :half]
            pair_rows[f, y, :, half:] = other[:, half:]
            pair_time[f + 1, y, :, :half] = window[:, :half]
            pair_time[f, y, :, half:] = other[:, half:]

    sums = []
    cells = height * width
    for f in range(outs):
        taps = [
            pair_rows[f, :height],
            pair_rows[f + 1, :height],
            pair_rows[f + 2, :height],
            pair_time[f + 1, 1:],
            pair_time[f + 3, 1:],
        ]
        stacked = jnp.concatenate([tap.reshape(cells, LANES) for tap in taps], axis=1)
        hidden = jnp.dot(stacked, in_w[...], preferred_element_type=jnp.float32) + in_b_ref[...]
        hid[f] = hidden.reshape(height, width, chans)
        sums.append(jnp.sum(hidden, axis=0, keepdims=True))
        sums.append(jnp.sum(hidden * hidden, axis=0, keepdims=True))
    per_group = chans // G
    down = lax.broadcasted_iota(jnp.int32, (chans, chans), 0) // per_group
    over = lax.broadcasted_iota(jnp.int32, (chans, chans), 1) // per_group
    same = jnp.where(down == over, 1.0, 0.0).astype(jnp.float32)
    grouped = jnp.dot(
        jnp.concatenate(sums, axis=0),
        same,
        precision=lax.Precision.HIGHEST,
        preferred_element_type=jnp.float32,
    ) / (cells * per_group)

    span_rows = rows_here + 2
    for f in range(outs):
        mean = grouped[2 * f : 2 * f + 1]
        var = grouped[2 * f + 1 : 2 * f + 2] - mean * mean
        scale = lax.rsqrt(var + 1e-06) * gain_ref[...]

        @pl.loop(0, span_rows)
        def _(y, f=f, mean=mean, scale=scale):
            row = row0 + y - 1
            inside = jnp.logical_and(row >= 0, row < height)
            value = hid[f, jnp.clip(row, 0, height - 1)]
            value = (value - mean) * scale + nbias_ref[...]
            keep = jnp.where(inside, keep_own if f < CF else 1.0, 0.0)
            value = 0.5 * value * (1.0 + jnp.tanh(0.5 * value)) * keep
            nil = jnp.zeros((1, chans), jnp.float32)
            left = jnp.concatenate([nil, value[:-1]], axis=0)
            right = jnp.concatenate([value[1:], nil], axis=0)
            act[f, y, :, :chans] = left.astype(jnp.bfloat16)
            act[f, y, :, chans : 2 * chans] = value.astype(jnp.bfloat16)
            act[f, y, :, 2 * chans :] = right.astype(jnp.bfloat16)

    many = CF * rows_here * width
    total = hid[pl.ds(outs - CF, CF), pl.ds(row0, rows_here)].reshape(many, chans) + mid_b_ref[...]
    for t in range(3):
        for i in range(3):
            tap = 3 * t + i
            copies[tap].wait()
            cells_in = act[t : t + CF, i : i + rows_here].reshape(many, 3 * chans)
            weight = mid_w[3 * tap : 3 * tap + 3].reshape(3 * chans, chans)
            total = total + jnp.dot(cells_in, weight, preferred_element_type=jnp.float32)
    out_ref[...] = total.astype(jnp.bfloat16).reshape(CF, rows_here, width, chans)


def decode(counts, frames, rows_here, in_weight, in_bias, norm_gain, norm_bias, mid_weight, mid_bias):
    frames_in, height, blocks, _ = frames.shape
    chans = in_weight.shape[1]
    outs = frames_in - 2
    vmem = pl.BlockSpec(memory_space=pltpu.VMEM)
    return pl.pallas_call(
        functools.partial(decode_kernel, rows_here),
        out_shape=jax.ShapeDtypeStruct((CF, rows_here, W, chans), jnp.bfloat16),
        in_specs=[pl.BlockSpec(memory_space=pltpu.SMEM)] + [vmem] * 6 + [pl.BlockSpec(memory_space=pl.ANY)],
        out_specs=vmem,
        scratch_shapes=[
            pltpu.VMEM(mid_weight.shape, jnp.bfloat16),
            pltpu.VMEM((5 * LANES, chans), jnp.bfloat16),
            pltpu.VMEM((frames_in, height + 1, W, LANES), jnp.bfloat16),
            pltpu.VMEM((frames_in + 1, height + 1, W, LANES), jnp.bfloat16),
            pltpu.VMEM((outs, height, W, chans), jnp.float32),
            pltpu.VMEM((outs, rows_here + 2, W, 3 * chans), jnp.bfloat16),
            pltpu.SemaphoreType.DMA((9,)),
        ],
        compiler_params=pltpu.CompilerParams(vmem_limit_bytes=58 * 1024 * 1024),
        name="span_decode",
    )(
        counts,
        frames,
        in_weight,
        in_bias[None],
        norm_gain[None],
        norm_bias[None],
        mid_bias[None],
        mid_weight,
    )


def local(
    latents,
    dispatch_plan,
    span_counts,
    in_weight,
    in_bias,
    norm_gain,
    norm_bias,
    mid_weight,
    mid_bias,
):
    rows_here = latents.shape[2]
    chans = mid_weight.shape[2]
    arrived = exchange(latents, dispatch_plan)
    row_n, req_n = arrived.shape[:2]
    frames = arrived.transpose(2, 3, 0, 4, 1, 5).reshape(
        DEPTH * CF, row_n * rows_here, W * C_LAT // LANES, LANES
    )
    mixed = decode(
        span_counts, frames, rows_here, in_weight, in_bias, norm_gain, norm_bias, mid_weight, mid_bias
    )
    return mixed.reshape(1, CF, rows_here, W * chans)


def solution(mesh):
    placed = (
        P("groups", None, "row", "req"),
        P("groups"),
        P("groups"),
        P(),
        P(),
        P(),
        P(),
        P(),
        P(),
    )
    return jax.shard_map(
        local,
        mesh=mesh,
        in_specs=placed,
        out_specs=P(("groups", "req"), None, "row", None),
        check_vma=False,
    )
```

time: 83.1 us -> 44.3 us (0.53)
  the two profiles are of different devices: /device:TPU:14 before, /device:TPU:0 now
where the time goes in v1:
time: 44.3 us; the launch traced here: 44 us
  Pallas kernels  35.3 us (80%)
  local copies, waits for them, and re-layouts  8.67 us (20%)
    pallas_call x1, Pallas kernels, decode(): pl.pallas_call(functools.partial(decode_kernel, rows_here), out_shape=jax...  23.2 us
    pallas_call x1, Pallas kernels, exchange(): pl.pallas_call(functools.partial(exchange_kernel, req_n, row_n), out_shap...  12.1 us
    reshape x1, local copies, waits for them, and re-layouts, local(): return mixed.reshape(1, CF, rows_here, W * chans)  1.83 us
    broadcast_in_dim x1, local copies, waits for them, and re-layouts, decode(): norm_bias[None]  1.27 us
    broadcast_in_dim x1, local copies, waits for them, and re-layouts, decode(): mid_bias[None]  1.26 us
    broadcast_in_dim x1, local copies, waits for them, and re-layouts, decode(): in_bias[None]  1.26 us
    broadcast_in_dim x1, local copies, waits for them, and re-layouts, decode(): norm_gain[None]  1.23 us
    transpose x1, local copies, waits for them, and re-layouts, local(): arrived.transpose(2, 3, 0, 4, 1, 5)  0.93 us

profile of v1, /device:TPU:0, one launch (start us, length us, event | category | flops | bytes accessed | tf_op | source)
XLA Modules:
  0.0 44.0 jit_solution(7744955064533126966)
XLA Ops:
  0.0 1.3 %broadcast_in_dim.12.in_b_ref = f32[1,384]{1,0:T(1,128)} reshape(f32[384]{0:T(512)} %param.13) | data formatting | bytes 3072 | tf_op jit(solution)/shard_map/broadcast_in_dim | solution.py:253
  1.3 1.2 %broadcast_in_dim.13.gain_ref = f32[1,384]{1,0:T(1,128)} reshape(f32[384]{0:T(512)} %param.14) | data formatting | bytes 3072 | tf_op jit(solution)/shard_map/broadcast_in_dim | solution.py:254
  2.5 1.3 %broadcast_in_dim.14.nbias_ref = f32[1,384]{1,0:T(1,128)} reshape(f32[384]{0:T(512)} %param.15) | data formatting | bytes 3072 | tf_op jit(solution)/shard_map/broadcast_in_dim | solution.py:255
  3.8 1.3 %broadcast_in_dim.15.mid_b_ref = f32[1,384]{1,0:T(1,128)} reshape(f32[384]{0:T(512)} %param.17) | data formatting | bytes 3072 | tf_op jit(solution)/shard_map/broadcast_in_dim | solution.py:256
  5.0 12.1 %span_exchange.1 = bf16[2,8,3,2,2,320]{5,4,3,2,1,0:T(2,128)(2,1)} custom-call(s32[8]{0:T(128)} %plan_ref.1, bf16[8,2,2,320]{3,2,1,0:T(2,128)(2,1)} %lat_ref.1), custom_call_target="tpu_custom_call" | custom-call | tf_op jit(solution)/shard_map/span_exchange/pallas_call | solution.py:59
  17.1 0.9 %copy.11 = bf16[3,2,2,2,8,320]{5,4,3,2,1,0:T(8,128)(2,1)S(1)} copy(bf16[3,2,2,2,8,320]{5,3,1,0,4,2:T(2,128)(2,1)} %bitcast.5) | data formatting | bytes 245760 | tf_op jit(solution)/shard_map/transpose | solution.py:276
  18.1 0.9 %reshape.6.x_ref = bf16[6,4,20,128]{3,2,1,0:T(8,128)(2,1)} reshape(bf16[3,2,2,2,8,320]{5,4,3,2,1,0:T(8,128)(2,1)S(1)} %copy.11) | data formatting | bytes 245760 | tf_op jit(solution)/shard_map/reshape | solution.py:276
  19.0 23.2 %span_decode.1 = bf16[2,2,160,384]{3,2,1,0:T(8,128)(2,1)} custom-call(s32[4]{0:T(128)} %counts_ref.1, bf16[6,4,20,128]{3,2,1,0:T(8,128)(2,1)} %reshape.6.x_ref, bf16[432,384]{1,0:T(8,128)(2,1)} %in_w_ref.1, f32[1,384]{1,0:T(1,128)} %broadcast_in_dim.12.in_b_ref, f32[1,384]{1,0:T(1,128)} %broadcast_in_dim.13.gain_ref, f32[1,384]{1,0:T(1,128)} %broadcast_in_dim.14.nbias_ref, ...), custom_call_target="tpu_custom_call" | custom-call | tf_op jit(solution)/shard_map/span_decode/pallas_call | solution.py:233
  42.1 1.8 %reshape.7 = bf16[1,2,2,61440]{3,2,1,0:T(2,128)(2,1)} reshape(bf16[2,2,160,384]{3,2,1,0:T(8,128)(2,1)} %span_decode.1) | data formatting | bytes 983040 | tf_op jit(solution)/shard_map/reshape | solution.py:282

commit v2 on v1

--- a/solution.py
+++ b/solution.py
@@ -93,10 +93,17 @@
     act,
     sems,
 ):
-    frames_in, height, blocks, _ = x_ref.shape
+    row_n, req_n = x_ref.shape[:2]
+    frames_in = DEPTH * CF
+    height = row_n * rows_here
+    width = req_n * x_ref.shape[5] // C_LAT
+    blocks = width * C_LAT // LANES
     chans = in_w_ref.shape[1]
     outs = frames_in - 2
-    width = blocks * (LANES // C_LAT)
+    in_b = in_b_ref[...].reshape(1, chans)
+    gain = gain_ref[...].reshape(1, chans)
+    nbias = nbias_ref[...].reshape(1, chans)
+    mid_b = mid_b_ref[...].reshape(1, chans)
     me = lax.axis_index("req")
     row0 = lax.axis_index("row") * rows_here
 
@@ -145,26 +152,37 @@
     bits = [lax.rem(place // (1 << n), 2) == 1 for n in range(3)]
     edge = jnp.zeros((8, LANES), jnp.float32)
 
+    def place_row(f, y, line):
+        spread = jnp.concatenate(
+            [
+                jnp.broadcast_to(line[:, LANES * b : LANES * (b + 1)], (8, LANES))
+                for b in range(blocks)
+            ],
+            axis=0,
+        )
+        turned = jnp.where(bits[0], spread, pltpu.roll(spread, C_LAT, 1))
+        turned = jnp.where(bits[1], pltpu.roll(turned, LANES - 2 * C_LAT, 1), turned)
+        turned = jnp.where(bits[2], pltpu.roll(turned, LANES - 4 * C_LAT, 1), turned)
+        before = jnp.concatenate([edge, turned[:-8]], axis=0)
+        after = jnp.concatenate([turned[8:], edge], axis=0)
+        window = jnp.where(low, before, jnp.where(high, after, turned))
+        other = pltpu.roll(window, half, 1).astype(jnp.bfloat16)
+        window = window.astype(jnp.bfloat16)
+        pair_rows[f, y + 1, :, :half] = window[:, :half]
+        pair_rows[f, y, :, half:] = other[:, half:]
+        pair_time[f + 1, y, :, :half] = window[:, :half]
+        pair_time[f, y, :, half:] = other[:, half:]
+
     @pl.loop(0, frames_in)
     def _(f):
         keep = jnp.where(f < CF, keep_prev, jnp.where(f < 2 * CF, keep_own, 1.0))
 
-        @pl.loop(0, height)
-        def _(y):
-            cells = x_ref[f, y].astype(jnp.float32) * keep
-            spread = jnp.broadcast_to(cells[:, None, :], (blocks, 8, LANES)).reshape(width, LANES)
-            turned = jnp.where(bits[0], spread, pltpu.roll(spread, C_LAT, 1))
-            turned = jnp.where(bits[1], pltpu.roll(turned, LANES - 2 * C_LAT, 1), turned)
-            turned = jnp.where(bits[2], pltpu.roll(turned, LANES - 4 * C_LAT, 1), turned)
-            before = jnp.concatenate([edge, turned[:-8]], axis=0)
-            after = jnp.concatenate([turned[8:], edge], axis=0)
-            window = jnp.where(low, before, jnp.where(high, after, turned))
-            other = pltpu.roll(window, half, 1).astype(jnp.bfloat16)
-            window = window.astype(jnp.bfloat16)
-            pair_rows[f, y + 1, :, :half] = window[:, :half]
-            pair_rows[f, y, :, half:] = other[:, half:]
-            pair_time[f + 1, y, :, :half] = window[:, :half]
-            pair_time[f, y, :, half:] = other[:, half:]
+        @pl.loop(0, row_n)
+        def _(r):
+            shards = [x_ref[r, q, f // CF, f % CF].astype(jnp.float32) for q in range(req_n)]
+            merged = jnp.concatenate(shards, axis=1) * keep
+            for here in range(rows_here):
+                place_row(f, r * rows_here + here, merged[here : here + 1])
 
     sums = []
     cells = height * width
@@ -177,7 +195,7 @@
             pair_time[f + 3, 1:],
         ]
         stacked = jnp.concatenate([tap.reshape(cells, LANES) for tap in taps], axis=1)
-        hidden = jnp.dot(stacked, in_w[...], preferred_element_type=jnp.float32) + in_b_ref[...]
+        hidden = jnp.dot(stacked, in_w[...], preferred_element_type=jnp.float32) + in_b
         hid[f] = hidden.reshape(height, width, chans)
         sums.append(jnp.sum(hidden, axis=0, keepdims=True))
         sums.append(jnp.sum(hidden * hidden, axis=0, keepdims=True))
@@ -196,14 +214,14 @@
     for f in range(outs):
         mean = grouped[2 * f : 2 * f + 1]
         var = grouped[2 * f + 1 : 2 * f + 2] - mean * mean
-        scale = lax.rsqrt(var + 1e-06) * gain_ref[...]
+        scale = lax.rsqrt(var + 1e-06) * gain
 
         @pl.loop(0, span_rows)
         def _(y, f=f, mean=mean, scale=scale):
             row = row0 + y - 1
             inside = jnp.logical_and(row >= 0, row < height)
             value = hid[f, jnp.clip(row, 0, height - 1)]
-            value = (value - mean) * scale + nbias_ref[...]
+            value = (value - mean) * scale + nbias
             keep = jnp.where(inside, keep_own if f < CF else 1.0, 0.0)
             value = 0.5 * value * (1.0 + jnp.tanh(0.5 * value)) * keep
             nil = jnp.zeros((1, chans), jnp.float32)
@@ -214,7 +232,7 @@
             act[f, y, :, 2 * chans :] = right.astype(jnp.bfloat16)
 
     many = CF * rows_here * width
-    total = hid[pl.ds(outs - CF, CF), pl.ds(row0, rows_here)].reshape(many, chans) + mid_b_ref[...]
+    total = hid[pl.ds(outs - CF, CF), pl.ds(row0, rows_here)].reshape(many, chans) + mid_b
     for t in range(3):
         for i in range(3):
             tap = 3 * t + i
@@ -226,7 +244,8 @@
 
 
 def decode(counts, frames, rows_here, in_weight, in_bias, norm_gain, norm_bias, mid_weight, mid_bias):
-    frames_in, height, blocks, _ = frames.shape
+    frames_in = DEPTH * CF
+    height = frames.shape[0] * rows_here
     chans = in_weight.shape[1]
     outs = frames_in - 2
     vmem = pl.BlockSpec(memory_space=pltpu.VMEM)
@@ -250,10 +269,10 @@
         counts,
         frames,
         in_weight,
-        in_bias[None],
-        norm_gain[None],
-        norm_bias[None],
-        mid_bias[None],
+        in_bias,
+        norm_gain,
+        norm_bias,
+        mid_bias,
         mid_weight,
     )
 
@@ -272,12 +291,8 @@
     rows_here = latents.shape[2]
     chans = mid_weight.shape[2]
     arrived = exchange(latents, dispatch_plan)
-    row_n, req_n = arrived.shape[:2]
-    frames = arrived.transpose(2, 3, 0, 4, 1, 5).reshape(
-        DEPTH * CF, row_n * rows_here, W * C_LAT // LANES, LANES
-    )
     mixed = decode(
-        span_counts, frames, rows_here, in_weight, in_bias, norm_gain, norm_bias, mid_weight, mid_bias
+        span_counts, arrived, rows_here, in_weight, in_bias, norm_gain, norm_bias, mid_weight, mid_bias
     )
     return mixed.reshape(1, CF, rows_here, W * chans)
 

time: 44.3 us -> 34.7 us (0.78)
  local copies, waits for them, and re-layouts: 8.67 us -> 1.83 us
  Pallas kernels: 35.3 us -> 32.7 us
    broadcast_in_dim x4 -> x0, local copies, waits for them, and re-layouts: 5.02 us -> none  [the longest x1 1.27 us: decode(): norm_bias[None]]
    pallas_call x1, Pallas kernels: 23.2 us -> 20.5 us  [decode(): pl.pallas_call(functools.partial(decode_kernel, rows_here), out_shape=jax...]
    transpose x1 -> x0, local copies, waits for them, and re-layouts: 0.93 us -> none  [local(): arrived.transpose(2, 3, 0, 4, 1, 5)]
    reshape x1 -> x0, local copies, waits for them, and re-layouts: 0.88 us -> none  [local(): arrived.transpose(2, 3, 0, 4, 1, 5)]
where the time goes in v2:
time: 34.7 us; the launch traced here: 34.5 us
  Pallas kernels  32.7 us (94%)
  local copies, waits for them, and re-layouts  1.83 us (5%)
    pallas_call x1, Pallas kernels, decode(): pl.pallas_call(functools.partial(decode_kernel, rows_here), out_shape=jax...  20.5 us
    pallas_call x1, Pallas kernels, exchange(): pl.pallas_call(functools.partial(exchange_kernel, req_n, row_n), out_shap...  12.1 us
    reshape x1, local copies, waits for them, and re-layouts, local(): return mixed.reshape(1, CF, rows_here, W * chans)  1.83 us

profile of v2, /device:TPU:0, one launch (start us, length us, event | category | flops | bytes accessed | tf_op | source)
XLA Modules:
  0.0 34.5 jit_solution(6804348624124408501)
XLA Ops:
  0.0 12.1 %span_exchange.1.x_ref = bf16[2,8,3,2,2,320]{5,4,3,2,1,0:T(2,128)(2,1)} custom-call(s32[8]{0:T(128)} %plan_ref.1, bf16[8,2,2,320]{3,2,1,0:T(2,128)(2,1)} %lat_ref.1), custom_call_target="tpu_custom_call" | custom-call | tf_op jit(solution)/shard_map/span_exchange/pallas_call | solution.py:59
  12.1 20.5 %span_decode.1 = bf16[2,2,160,384]{3,2,1,0:T(8,128)(2,1)} custom-call(s32[4]{0:T(128)} %counts_ref.1, bf16[2,8,3,2,2,320]{5,4,3,2,1,0:T(2,128)(2,1)} %span_exchange.1.x_ref, bf16[432,384]{1,0:T(8,128)(2,1)} %in_w_ref.1, f32[384]{0:T(512)} %in_b_ref.1, f32[384]{0:T(512)} %gain_ref.1, f32[384]{0:T(512)} %nbias_ref.1, f32[384]{0:T(512)} %mid_b_ref.1, ...), custom_call_target="tpu_custom_call" | custom-call | tf_op jit(solution)/shard_map/span_decode/pallas_call | solution.py:252
  32.7 1.8 %reshape.3 = bf16[1,2,2,61440]{3,2,1,0:T(2,128)(2,1)} reshape(bf16[2,2,160,384]{3,2,1,0:T(8,128)(2,1)} %span_decode.1) | data formatting | bytes 983040 | tf_op jit(solution)/shard_map/reshape | solution.py:297

commit v3 on v2

--- a/solution.py
+++ b/solution.py
@@ -16,75 +16,29 @@
 MESH = pl.DeviceIdType.MESH
 
 
-def exchange_kernel(req_n, row_n, plan_ref, lat_ref, out_ref, sel, send_sems, recv_sems):
-    me_req = lax.axis_index("req")
-    me_row = lax.axis_index("row")
-    total = req_n * row_n
-    flat = me_row * req_n + me_req
-    barrier = pltpu.get_barrier_semaphore()
-
-    def place(k):
-        target = lax.rem(flat + k, total)
-        return {"row": target // req_n, "req": lax.rem(target, req_n)}
-
-    for k in range(1, total):
-        pl.semaphore_signal(barrier, inc=1, device_id=place(k), device_id_type=MESH)
-    for d in range(DEPTH - 1):
-        sel[d] = jnp.zeros_like(sel[d])
-    for d in range(req_n):
-        sel[d + DEPTH - 1] = lat_ref[plan_ref[d]]
-    pl.semaphore_wait(barrier, total - 1)
-    copies = []
-    for k in range(1, total):
-        where = place(k)
-        copy = pltpu.make_async_remote_copy(
-            src_ref=sel.at[pl.ds(where["req"], DEPTH)],
-            dst_ref=out_ref.at[me_row, me_req],
-            send_sem=send_sems.at[k],
-            recv_sem=recv_sems.at[k],
-            device_id=where,
-            device_id_type=MESH,
-        )
-        copy.start()
-        copies.append(copy)
-    out_ref[me_row, me_req] = sel[pl.ds(me_req, DEPTH)]
-    for copy in copies:
-        copy.wait()
-
-
-def exchange(latents, plan):
-    req_n = lax.axis_size("req")
-    row_n = lax.axis_size("row")
-    slots, frames, rows, lanes = latents.shape
-    return pl.pallas_call(
-        functools.partial(exchange_kernel, req_n, row_n),
-        out_shape=jax.ShapeDtypeStruct((row_n, req_n, DEPTH, frames, rows, lanes), latents.dtype),
-        in_specs=[
-            pl.BlockSpec(memory_space=pltpu.SMEM),
-            pl.BlockSpec(memory_space=pltpu.VMEM),
-        ],
-        out_specs=pl.BlockSpec(memory_space=pltpu.VMEM),
-        scratch_shapes=[
-            pltpu.VMEM((req_n + DEPTH - 1, frames, rows, lanes), latents.dtype),
-            pltpu.SemaphoreType.DMA((req_n * row_n,)),
-            pltpu.SemaphoreType.DMA((req_n * row_n,)),
-        ],
-        compiler_params=pltpu.CompilerParams(collective_id=0, has_side_effects=True),
-        name="span_exchange",
-    )(plan, latents)
-
-
-def decode_kernel(
-    rows_here,
+def span_kernel(
+    req_n,
+    row_n,
+    lat_hbm,
+    plan_hbm,
+    counts_hbm,
+    in_w_hbm,
+    in_b_hbm,
+    gain_hbm,
+    nbias_hbm,
+    mid_w_hbm,
+    mid_b_hbm,
+    out_ref,
+    lat_ref,
+    plan_ref,
     counts_ref,
-    x_ref,
     in_w_ref,
     in_b_ref,
     gain_ref,
     nbias_ref,
     mid_b_ref,
-    mid_w_hbm,
-    out_ref,
+    sel,
+    x_ref,
     mid_w,
     in_w,
     pair_rows,
@@ -92,8 +46,71 @@
     hid,
     act,
     sems,
+    send_sems,
+    recv_sems,
 ):
-    row_n, req_n = x_ref.shape[:2]
+    me = lax.axis_index("req")
+    me_row = lax.axis_index("row")
+    devices = req_n * row_n
+    flat = me_row * req_n + me
+    rows_here = lat_ref.shape[2]
+    row0 = me_row * rows_here
+
+    def peer(k):
+        target = lax.rem(flat + k, devices)
+        return {"row": target // req_n, "req": lax.rem(target, req_n)}
+
+    barrier = pltpu.get_barrier_semaphore()
+    for k in range(1, devices):
+        pl.semaphore_signal(barrier, inc=1, device_id=peer(k), device_id_type=MESH)
+    loads = [
+        pltpu.make_async_copy(source, target, sems.at[9 + n])
+        for n, (source, target) in enumerate(
+            (
+                (plan_hbm, plan_ref),
+                (lat_hbm, lat_ref),
+                (counts_hbm, counts_ref),
+                (in_w_hbm, in_w_ref),
+                (in_b_hbm, in_b_ref),
+                (gain_hbm, gain_ref),
+                (nbias_hbm, nbias_ref),
+                (mid_b_hbm, mid_b_ref),
+            )
+        )
+    ]
+    for load in loads:
+        load.start()
+    copies = []
+    for tap in range(9):
+        copy = pltpu.make_async_copy(
+            mid_w_hbm.at[pl.ds(3 * tap, 3)], mid_w.at[pl.ds(3 * tap, 3)], sems.at[tap]
+        )
+        copy.start()
+        copies.append(copy)
+    loads[0].wait()
+    loads[1].wait()
+    for d in range(DEPTH - 1):
+        sel[d] = jnp.zeros_like(sel[d])
+    for d in range(req_n):
+        sel[d + DEPTH - 1] = lat_ref[plan_ref[d]]
+    pl.semaphore_wait(barrier, devices - 1)
+    sends = []
+    for k in range(1, devices):
+        where = peer(k)
+        send = pltpu.make_async_remote_copy(
+            src_ref=sel.at[pl.ds(where["req"], DEPTH)],
+            dst_ref=x_ref.at[me_row, me],
+            send_sem=send_sems.at[k],
+            recv_sem=recv_sems.at[k],
+            device_id=where,
+            device_id_type=MESH,
+        )
+        send.start()
+        sends.append(send)
+    x_ref[me_row, me] = sel[pl.ds(me, DEPTH)]
+    for load in loads[2:]:
+        load.wait()
+
     frames_in = DEPTH * CF
     height = row_n * rows_here
     width = req_n * x_ref.shape[5] // C_LAT
@@ -104,17 +121,6 @@
     gain = gain_ref[...].reshape(1, chans)
     nbias = nbias_ref[...].reshape(1, chans)
     mid_b = mid_b_ref[...].reshape(1, chans)
-    me = lax.axis_index("req")
-    row0 = lax.axis_index("row") * rows_here
-
-    copies = []
-    for tap in range(9):
-        copy = pltpu.make_async_copy(
-            mid_w_hbm.at[pl.ds(3 * tap, 3)], mid_w.at[pl.ds(3 * tap, 3)], sems.at[tap]
-        )
-        copy.start()
-        copies.append(copy)
-
     def keep_of(d):
         start = jnp.int32(0)
         first = d <= 0
@@ -172,6 +178,9 @@
         pair_rows[f, y, :, half:] = other[:, half:]
         pair_time[f + 1, y, :, :half] = window[:, :half]
         pair_time[f, y, :, half:] = other[:, half:]
+
+    for send in sends:
+        send.wait()
 
     @pl.loop(0, frames_in)
     def _(f):
@@ -224,56 +233,81 @@
             value = (value - mean) * scale + nbias
             keep = jnp.where(inside, keep_own if f < CF else 1.0, 0.0)
             value = 0.5 * value * (1.0 + jnp.tanh(0.5 * value)) * keep
-            nil = jnp.zeros((1, chans), jnp.float32)
-            left = jnp.concatenate([nil, value[:-1]], axis=0)
-            right = jnp.concatenate([value[1:], nil], axis=0)
-            act[f, y, :, :chans] = left.astype(jnp.bfloat16)
-            act[f, y, :, chans : 2 * chans] = value.astype(jnp.bfloat16)
-            act[f, y, :, 2 * chans :] = right.astype(jnp.bfloat16)
+            act[f, y] = value.astype(jnp.bfloat16)
 
     many = CF * rows_here * width
-    total = hid[pl.ds(outs - CF, CF), pl.ds(row0, rows_here)].reshape(many, chans) + mid_b
+    for copy in copies:
+        copy.wait()
+    slabs = []
+    weights = []
     for t in range(3):
         for i in range(3):
-            tap = 3 * t + i
-            copies[tap].wait()
-            cells_in = act[t : t + CF, i : i + rows_here].reshape(many, 3 * chans)
-            weight = mid_w[3 * tap : 3 * tap + 3].reshape(3 * chans, chans)
-            total = total + jnp.dot(cells_in, weight, preferred_element_type=jnp.float32)
-    out_ref[...] = total.astype(jnp.bfloat16).reshape(CF, rows_here, width, chans)
-
-
-def decode(counts, frames, rows_here, in_weight, in_bias, norm_gain, norm_bias, mid_weight, mid_bias):
+            tap = 3 * (3 * t + i)
+            slabs.append(act[t : t + CF, i : i + rows_here].reshape(many, chans))
+            weights.append(jnp.concatenate([mid_w[tap + j] for j in range(3)], axis=1))
+    columns = jnp.dot(
+        jnp.concatenate(slabs, axis=1),
+        jnp.concatenate(weights, axis=0),
+        preferred_element_type=jnp.float32,
+    ).reshape(CF * rows_here, width, 3 * chans)
+    nil = jnp.zeros((1, chans), jnp.float32)
+    for f in range(CF):
+        for y in range(rows_here):
+            part = columns[f * rows_here + y]
+            total = hid[outs - CF + f, row0 + y] + mid_b + part[:, chans : 2 * chans]
+            total = total + jnp.concatenate([nil, part[:-1, :chans]], axis=0)
+            total = total + jnp.concatenate([part[1:, 2 * chans :], nil], axis=0)
+            out_ref[f, y] = total.astype(jnp.bfloat16)
+
+
+def spans(latents, dispatch_plan, span_counts, in_weight, in_bias, norm_gain, norm_bias, mid_weight, mid_bias):
+    req_n = lax.axis_size("req")
+    row_n = lax.axis_size("row")
+    frames, rows_here, lanes = latents.shape[1:]
+    chans = in_weight.shape[1]
     frames_in = DEPTH * CF
-    height = frames.shape[0] * rows_here
-    chans = in_weight.shape[1]
     outs = frames_in - 2
-    vmem = pl.BlockSpec(memory_space=pltpu.VMEM)
+    height = row_n * rows_here
     return pl.pallas_call(
-        functools.partial(decode_kernel, rows_here),
+        functools.partial(span_kernel, req_n, row_n),
         out_shape=jax.ShapeDtypeStruct((CF, rows_here, W, chans), jnp.bfloat16),
-        in_specs=[pl.BlockSpec(memory_space=pltpu.SMEM)] + [vmem] * 6 + [pl.BlockSpec(memory_space=pl.ANY)],
-        out_specs=vmem,
+        in_specs=[pl.BlockSpec(memory_space=pl.ANY)] * 9,
+        out_specs=pl.BlockSpec(memory_space=pltpu.VMEM),
         scratch_shapes=[
+            pltpu.VMEM(latents.shape, latents.dtype),
+            pltpu.SMEM(dispatch_plan.shape, jnp.int32),
+            pltpu.SMEM(span_counts.shape, jnp.int32),
+            pltpu.VMEM(in_weight.shape, in_weight.dtype),
+            pltpu.VMEM((chans,), jnp.float32),
+            pltpu.VMEM((chans,), jnp.float32),
+            pltpu.VMEM((chans,), jnp.float32),
+            pltpu.VMEM((chans,), jnp.float32),
+            pltpu.VMEM((req_n + DEPTH - 1, frames, rows_here, lanes), latents.dtype),
+            pltpu.VMEM((row_n, req_n, DEPTH, frames, rows_here, lanes), latents.dtype),
             pltpu.VMEM(mid_weight.shape, jnp.bfloat16),
             pltpu.VMEM((5 * LANES, chans), jnp.bfloat16),
             pltpu.VMEM((frames_in, height + 1, W, LANES), jnp.bfloat16),
             pltpu.VMEM((frames_in + 1, height + 1, W, LANES), jnp.bfloat16),
             pltpu.VMEM((outs, height, W, chans), jnp.float32),
-            pltpu.VMEM((outs, rows_here + 2, W, 3 * chans), jnp.bfloat16),
-            pltpu.SemaphoreType.DMA((9,)),
+            pltpu.VMEM((outs, rows_here + 2, W, chans), jnp.bfloat16),
+            pltpu.SemaphoreType.DMA((17,)),
+            pltpu.SemaphoreType.DMA((req_n * row_n,)),
+            pltpu.SemaphoreType.DMA((req_n * row_n,)),
         ],
-        compiler_params=pltpu.CompilerParams(vmem_limit_bytes=58 * 1024 * 1024),
-        name="span_decode",
+        compiler_params=pltpu.CompilerParams(
+            collective_id=0, has_side_effects=True, vmem_limit_bytes=58 * 1024 * 1024
+        ),
+        name="spans",
     )(
-        counts,
-        frames,
+        latents,
+        dispatch_plan,
+        span_counts,
         in_weight,
         in_bias,
         norm_gain,
         norm_bias,
+        mid_weight,
         mid_bias,
-        mid_weight,
     )
 
 
@@ -290,9 +324,16 @@
 ):
     rows_here = latents.shape[2]
     chans = mid_weight.shape[2]
-    arrived = exchange(latents, dispatch_plan)
-    mixed = decode(
-        span_counts, arrived, rows_here, in_weight, in_bias, norm_gain, norm_bias, mid_weight, mid_bias
+    mixed = spans(
+        latents,
+        dispatch_plan,
+        span_counts,
+        in_weight,
+        in_bias,
+        norm_gain,
+        norm_bias,
+        mid_weight,
+        mid_bias,
     )
     return mixed.reshape(1, CF, rows_here, W * chans)
 

time: 34.7 us -> 30 us (0.86)
  Pallas kernels: 32.7 us -> 28 us
    pallas_call x2 -> x1, Pallas kernels: 32.7 us -> 28 us  [spans(): pl.pallas_call(functools.partial(span_kernel, req_n, row_n), out_shape=ja...]
where the time goes in v3:
time: 30 us; the launch traced here: 29.9 us
  Pallas kernels  28 us (93%)
  local copies, waits for them, and re-layouts  1.83 us (6%)
    pallas_call x1, Pallas kernels, spans(): pl.pallas_call(functools.partial(span_kernel, req_n, row_n), out_shape=ja...  28 us
    reshape x1, local copies, waits for them, and re-layouts, local(): return mixed.reshape(1, CF, rows_here, W * chans)  1.83 us

profile of v3, /device:TPU:0, one launch (start us, length us, event | category | flops | bytes accessed | tf_op | source)
XLA Modules:
  0.0 29.9 jit_solution(10492528341015447070)
XLA Ops:
  0.0 28.0 %spans.1 = bf16[2,2,160,384]{3,2,1,0:T(8,128)(2,1)} custom-call(bf16[8,2,2,320]{3,2,1,0:T(2,128)(2,1)} %lat_hbm.1, s32[8]{0:T(128)} %plan_hbm.1, s32[4]{0:T(128)} %counts_hbm.1, bf16[432,384]{1,0:T(8,128)(2,1)} %in_w_hbm.1, f32[384]{0:T(512)} %in_b_hbm.1, f32[384]{0:T(512)} %gain_hbm.1, f32[384]{0:T(512)} %nbias_hbm.1, bf16[27,384,384]{2,1,0:T(8,128)(2,1)} %mid_w_hbm.1, ...), custom_call_target="tpu_custom_call" | custom-call | tf_op jit(solution)/shard_map/spans/pallas_call | solution.py:271
  28.0 1.8 %reshape.3 = bf16[1,2,2,61440]{3,2,1,0:T(2,128)(2,1)} reshape(bf16[2,2,160,384]{3,2,1,0:T(8,128)(2,1)} %spans.1) | data formatting | bytes 983040 | tf_op jit(solution)/shard_map/reshape | solution.py:338

commit v4 on v3

--- a/solution.py
+++ b/solution.py
@@ -45,6 +45,8 @@
     pair_time,
     hid,
     act,
+    lines,
+    fanned,
     sems,
     send_sems,
     recv_sems,
@@ -92,7 +94,8 @@
     for d in range(DEPTH - 1):
         sel[d] = jnp.zeros_like(sel[d])
     for d in range(req_n):
-        sel[d + DEPTH - 1] = lat_ref[plan_ref[d]]
+        span = lat_ref[plan_ref[d]].astype(jnp.float32)
+        sel[d + DEPTH - 1] = jnp.concatenate([span[f] for f in range(CF)], axis=1).astype(sel.dtype)
     pl.semaphore_wait(barrier, devices - 1)
     sends = []
     for k in range(1, devices):
@@ -113,7 +116,8 @@
 
     frames_in = DEPTH * CF
     height = row_n * rows_here
-    width = req_n * x_ref.shape[5] // C_LAT
+    lanes = x_ref.shape[4] // CF
+    width = req_n * lanes // C_LAT
     blocks = width * C_LAT // LANES
     chans = in_w_ref.shape[1]
     outs = frames_in - 2
@@ -151,47 +155,51 @@
     for y in range(height):
         pair_time[frames_in, y] = zero_slab
 
-    place = lax.broadcasted_iota(jnp.int32, (width, LANES), 0) % 8
-    lane = lax.broadcasted_iota(jnp.int32, (width, LANES), 1)
-    low = jnp.logical_and(place == 0, lane < C_LAT)
-    high = jnp.logical_and(place == 7, jnp.logical_and(lane >= 2 * C_LAT, lane < three))
-    bits = [lax.rem(place // (1 << n), 2) == 1 for n in range(3)]
-    edge = jnp.zeros((8, LANES), jnp.float32)
-
-    def place_row(f, y, line):
-        spread = jnp.concatenate(
-            [
-                jnp.broadcast_to(line[:, LANES * b : LANES * (b + 1)], (8, LANES))
-                for b in range(blocks)
-            ],
-            axis=0,
-        )
-        turned = jnp.where(bits[0], spread, pltpu.roll(spread, C_LAT, 1))
-        turned = jnp.where(bits[1], pltpu.roll(turned, LANES - 2 * C_LAT, 1), turned)
-        turned = jnp.where(bits[2], pltpu.roll(turned, LANES - 4 * C_LAT, 1), turned)
-        before = jnp.concatenate([edge, turned[:-8]], axis=0)
-        after = jnp.concatenate([turned[8:], edge], axis=0)
-        window = jnp.where(low, before, jnp.where(high, after, turned))
-        other = pltpu.roll(window, half, 1).astype(jnp.bfloat16)
-        window = window.astype(jnp.bfloat16)
-        pair_rows[f, y + 1, :, :half] = window[:, :half]
-        pair_rows[f, y, :, half:] = other[:, half:]
-        pair_time[f + 1, y, :, :half] = window[:, :half]
-        pair_time[f, y, :, half:] = other[:, half:]
+    lane = lax.broadcasted_iota(jnp.int32, (blocks, LANES), 1)
+    low = lane < C_LAT
+    high = jnp.logical_and(lane >= 2 * C_LAT, lane < three)
+    left = lane < half
+    nothing = jnp.zeros((1, LANES), jnp.float32)
+
+    def place_row(f, y, here):
+        cells = lines[pl.ds(here, blocks, stride=rows_here), :]
+        turned = [pltpu.roll(cells, (C_LAT - C_LAT * p) % LANES, 1) if p != 1 else cells for p in range(8)]
+        for p in range(8):
+            window = turned[p]
+            other = turned[(p + 4) % 8]
+            if p == 0:
+                before = jnp.concatenate([nothing, window[:-1]], axis=0)
+                window = jnp.where(low, before, window)
+                other = pltpu.roll(window, half, 1)
+            if p == 7:
+                after = jnp.concatenate([window[1:], nothing], axis=0)
+                window = jnp.where(high, after, window)
+                other = pltpu.roll(window, half, 1)
+            fanned[here, pl.ds(p, blocks, stride=8), :] = jnp.where(left, window, other)
+        both = fanned[here].astype(jnp.bfloat16)
+        pair_rows[f, y + 1, :, :half] = both[:, :half]
+        pair_rows[f, y, :, half:] = both[:, half:]
+        pair_time[f + 1, y, :, :half] = both[:, :half]
+        pair_time[f, y, :, half:] = both[:, half:]
 
     for send in sends:
         send.wait()
 
-    @pl.loop(0, frames_in)
-    def _(f):
-        keep = jnp.where(f < CF, keep_prev, jnp.where(f < 2 * CF, keep_own, 1.0))
+    @pl.loop(0, DEPTH)
+    def _(span):
+        keep = jnp.where(span == 0, keep_prev, jnp.where(span == 1, keep_own, 1.0))
 
         @pl.loop(0, row_n)
         def _(r):
-            shards = [x_ref[r, q, f // CF, f % CF].astype(jnp.float32) for q in range(req_n)]
-            merged = jnp.concatenate(shards, axis=1) * keep
-            for here in range(rows_here):
-                place_row(f, r * rows_here + here, merged[here : here + 1])
+            shards = [x_ref[r, q, span].astype(jnp.float32) * keep for q in range(req_n)]
+            for frame in range(CF):
+                merged = jnp.concatenate(
+                    [shard[:, frame * lanes : (frame + 1) * lanes] for shard in shards], axis=1
+                )
+                for b in range(blocks):
+                    lines[b * rows_here : (b + 1) * rows_here, :] = merged[:, b * LANES : (b + 1) * LANES]
+                for here in range(rows_here):
+                    place_row(span * CF + frame, r * rows_here + here, here)
 
     sums = []
     cells = height * width
@@ -229,11 +237,17 @@
         def _(y, f=f, mean=mean, scale=scale):
             row = row0 + y - 1
             inside = jnp.logical_and(row >= 0, row < height)
-            value = hid[f, jnp.clip(row, 0, height - 1)]
-            value = (value - mean) * scale + nbias
-            keep = jnp.where(inside, keep_own if f < CF else 1.0, 0.0)
-            value = 0.5 * value * (1.0 + jnp.tanh(0.5 * value)) * keep
-            act[f, y] = value.astype(jnp.bfloat16)
+            @pl.when(inside)
+            def _():
+                value = (hid[f, row] - mean) * scale + nbias
+                value = 0.5 * value * (1.0 + jnp.tanh(0.5 * value))
+                if f < CF:
+                    value = value * keep_own
+                act[f, y] = value.astype(jnp.bfloat16)
+
+            @pl.when(jnp.logical_not(inside))
+            def _():
+                act[f, y] = jnp.zeros((width, chans), jnp.bfloat16)
 
     many = CF * rows_here * width
     for copy in copies:
@@ -268,6 +282,7 @@
     frames_in = DEPTH * CF
     outs = frames_in - 2
     height = row_n * rows_here
+    blocks = W * C_LAT // LANES
     return pl.pallas_call(
         functools.partial(span_kernel, req_n, row_n),
         out_shape=jax.ShapeDtypeStruct((CF, rows_here, W, chans), jnp.bfloat16),
@@ -282,20 +297,22 @@
             pltpu.VMEM((chans,), jnp.float32),
             pltpu.VMEM((chans,), jnp.float32),
             pltpu.VMEM((chans,), jnp.float32),
-            pltpu.VMEM((req_n + DEPTH - 1, frames, rows_here, lanes), latents.dtype),
-            pltpu.VMEM((row_n, req_n, DEPTH, frames, rows_here, lanes), latents.dtype),
+            pltpu.VMEM((req_n + DEPTH - 1, rows_here, frames * lanes), latents.dtype),
+            pltpu.VMEM((row_n, req_n, DEPTH, rows_here, frames * lanes), latents.dtype),
             pltpu.VMEM(mid_weight.shape, jnp.bfloat16),
             pltpu.VMEM((5 * LANES, chans), jnp.bfloat16),
             pltpu.VMEM((frames_in, height + 1, W, LANES), jnp.bfloat16),
             pltpu.VMEM((frames_in + 1, height + 1, W, LANES), jnp.bfloat16),
             pltpu.VMEM((outs, height, W, chans), jnp.float32),
             pltpu.VMEM((outs, rows_here + 2, W, chans), jnp.bfloat16),
+            pltpu.VMEM((blocks * rows_here, LANES), jnp.float32),
+            pltpu.VMEM((rows_here, W, LANES), jnp.float32),
             pltpu.SemaphoreType.DMA((17,)),
             pltpu.SemaphoreType.DMA((req_n * row_n,)),
             pltpu.SemaphoreType.DMA((req_n * row_n,)),
         ],
         compiler_params=pltpu.CompilerParams(
-            collective_id=0, has_side_effects=True, vmem_limit_bytes=58 * 1024 * 1024
+            collective_id=0, has_side_effects=True, vmem_limit_bytes=58 << 20
         ),
         name="spans",
     )(

time: 30 us -> 26.6 us (0.89)
  Pallas kernels: 28 us -> 24.6 us
    pallas_call x1, Pallas kernels: 28 us -> 24.6 us  [spans(): pl.pallas_call(functools.partial(span_kernel, req_n, row_n), out_shape=ja...]
where the time goes in v4:
time: 26.6 us; the launch traced here: 26.4 us
  Pallas kernels  24.6 us (92%)
  local copies, waits for them, and re-layouts  1.83 us (7%)
    pallas_call x1, Pallas kernels, spans(): pl.pallas_call(functools.partial(span_kernel, req_n, row_n), out_shape=ja...  24.6 us
    reshape x1, local copies, waits for them, and re-layouts, local(): return mixed.reshape(1, CF, rows_here, W * chans)  1.83 us

profile of v4, /device:TPU:0, one launch (start us, length us, event | category | flops | bytes accessed | tf_op | source)
XLA Modules:
  0.0 26.4 jit_solution(10389497888031821167)
XLA Ops:
  0.0 24.6 %spans.1 = bf16[2,2,160,384]{3,2,1,0:T(8,128)(2,1)} custom-call(bf16[8,2,2,320]{3,2,1,0:T(2,128)(2,1)} %lat_hbm.1, s32[8]{0:T(128)} %plan_hbm.1, s32[4]{0:T(128)} %counts_hbm.1, bf16[432,384]{1,0:T(8,128)(2,1)} %in_w_hbm.1, f32[384]{0:T(512)} %in_b_hbm.1, f32[384]{0:T(512)} %gain_hbm.1, f32[384]{0:T(512)} %nbias_hbm.1, bf16[27,384,384]{2,1,0:T(8,128)(2,1)} %mid_w_hbm.1, ...), custom_call_target="tpu_custom_call" | custom-call | tf_op jit(solution)/shard_map/spans/pallas_call | solution.py:286
  24.6 1.8 %reshape.3 = bf16[1,2,2,61440]{3,2,1,0:T(2,128)(2,1)} reshape(bf16[2,2,160,384]{3,2,1,0:T(8,128)(2,1)} %spans.1) | data formatting | bytes 983040 | tf_op jit(solution)/shard_map/reshape | solution.py:355

commit v5 on v4

--- a/solution.py
+++ b/solution.py
@@ -283,10 +283,13 @@
     outs = frames_in - 2
     height = row_n * rows_here
     blocks = W * C_LAT // LANES
+    grant = mid_weight.size * 2 + 4 * chans * W * (outs * height + CF * rows_here)
+    grant += 2 * chans * W * outs * (rows_here + 2) + 4 * (frames_in + 1) * (height + 1) * W * LANES
+    grant += (8 << 20)
     return pl.pallas_call(
         functools.partial(span_kernel, req_n, row_n),
         out_shape=jax.ShapeDtypeStruct((CF, rows_here, W, chans), jnp.bfloat16),
-        in_specs=[pl.BlockSpec(memory_space=pl.ANY)] * 9,
+        in_specs=[pl.BlockSpec(memory_space=pltpu.HBM)] * 9,
         out_specs=pl.BlockSpec(memory_space=pltpu.VMEM),
         scratch_shapes=[
             pltpu.VMEM(latents.shape, latents.dtype),
@@ -312,19 +315,24 @@
             pltpu.SemaphoreType.DMA((req_n * row_n,)),
         ],
         compiler_params=pltpu.CompilerParams(
-            collective_id=0, has_side_effects=True, vmem_limit_bytes=58 << 20
+            collective_id=0, has_side_effects=True, vmem_limit_bytes=grant
         ),
         name="spans",
     )(
-        latents,
-        dispatch_plan,
-        span_counts,
-        in_weight,
-        in_bias,
-        norm_gain,
-        norm_bias,
-        mid_weight,
-        mid_bias,
+        *(
+            pltpu.with_memory_space_constraint(arg, pltpu.HBM)
+            for arg in (
+                latents,
+                dispatch_plan,
+                span_counts,
+                in_weight,
+                in_bias,
+                norm_gain,
+                norm_bias,
+                mid_weight,
+                mid_bias,
+            )
+        )
     )
 
 

time: 26.6 us -> 24.9 us (0.936)
  local copies, waits for them, and re-layouts: 1.83 us -> 0.86 us
  Pallas kernels: 24.6 us -> 23.8 us
    reshape x1, local copies, waits for them, and re-layouts: 1.83 us -> 0.86 us  [local(): return mixed.reshape(1, CF, rows_here, W * chans)]
    pallas_call x1, Pallas kernels: 24.6 us -> 23.8 us  [spans(): pl.pallas_call(functools.partial(span_kernel, req_n, row_n), out_shape=ja...]
where the time goes in v5:
time: 24.9 us; the launch traced here: 24.7 us
  Pallas kernels  23.8 us (96%)
  local copies, waits for them, and re-layouts  0.86 us (3%)
    pallas_call x1, Pallas kernels, spans(): pl.pallas_call(functools.partial(span_kernel, req_n, row_n), out_shape=ja...  23.8 us
    reshape x1, local copies, waits for them, and re-layouts, local(): return mixed.reshape(1, CF, rows_here, W * chans)  0.86 us

profile of v5, /device:TPU:0, one launch (start us, length us, event | category | flops | bytes accessed | tf_op | source)
XLA Modules:
  0.0 24.7 jit_solution(13976639268714299152)
XLA Ops:
  0.0 23.8 %spans.1 = bf16[2,2,160,384]{3,2,1,0:T(8,128)(2,1)S(1)} custom-call(bf16[8,2,2,320]{3,2,1,0:T(2,128)(2,1)} %lat_hbm.1, s32[8]{0:T(128)} %plan_hbm.1, s32[4]{0:T(128)} %counts_hbm.1, bf16[432,384]{1,0:T(8,128)(2,1)} %in_w_hbm.1, f32[384]{0:T(512)} %in_b_hbm.1, f32[384]{0:T(512)} %gain_hbm.1, f32[384]{0:T(512)} %nbias_hbm.1, bf16[27,384,384]{2,1,0:T(8,128)(2,1)} %mid_w_hbm.1, ...), custom_call_target="tpu_custom_call" | custom-call | tf_op jit(solution)/shard_map/spans/pallas_call | solution.py:289
  23.8 0.9 %reshape.3 = bf16[1,2,2,61440]{3,2,1,0:T(2,128)(2,1)} reshape(bf16[2,2,160,384]{3,2,1,0:T(8,128)(2,1)S(1)} %spans.1) | data formatting | bytes 983040 | tf_op jit(solution)/shard_map/reshape | solution.py:363

commit v6 on v5

--- a/solution.py
+++ b/solution.py
@@ -219,13 +219,15 @@
     per_group = chans // G
     down = lax.broadcasted_iota(jnp.int32, (chans, chans), 0) // per_group
     over = lax.broadcasted_iota(jnp.int32, (chans, chans), 1) // per_group
-    same = jnp.where(down == over, 1.0, 0.0).astype(jnp.float32)
-    grouped = jnp.dot(
-        jnp.concatenate(sums, axis=0),
-        same,
-        precision=lax.Precision.HIGHEST,
-        preferred_element_type=jnp.float32,
-    ) / (cells * per_group)
+    same = jnp.where(down == over, 1.0, 0.0).astype(jnp.bfloat16)
+    stats = jnp.concatenate(sums, axis=0)
+    parts = []
+    for _ in range(3):
+        part = stats.astype(jnp.bfloat16)
+        parts.append(part)
+        stats = stats - part.astype(jnp.float32)
+    grouped = sum(jnp.dot(part, same, preferred_element_type=jnp.float32) for part in reversed(parts))
+    grouped = grouped / (cells * per_group)
 
     span_rows = rows_here + 2
     for f in range(outs):

time: 24.9 us -> 25.2 us (1.012)
  Pallas kernels: 23.8 us -> 24.1 us
    pallas_call x1, Pallas kernels: 23.8 us -> 24.1 us  [spans(): pl.pallas_call(functools.partial(span_kernel, req_n, row_n), out_shape=ja...]
where the time goes in v6:
time: 25.2 us; the launch traced here: 25 us
  Pallas kernels  24.1 us (96%)
  local copies, waits for them, and re-layouts  0.86 us (3%)
    pallas_call x1, Pallas kernels, spans(): pl.pallas_call(functools.partial(span_kernel, req_n, row_n), out_shape=ja...  24.1 us
    reshape x1, local copies, waits for them, and re-layouts, local(): return mixed.reshape(1, CF, rows_here, W * chans)  0.86 us

profile of v6, /device:TPU:0, one launch (start us, length us, event | category | flops | bytes accessed | tf_op | source)
XLA Modules:
  0.0 25.0 jit_solution(7386940218819348963)
XLA Ops:
  0.0 24.1 %spans.1 = bf16[2,2,160,384]{3,2,1,0:T(8,128)(2,1)S(1)} custom-call(bf16[8,2,2,320]{3,2,1,0:T(2,128)(2,1)} %lat_hbm.1, s32[8]{0:T(128)} %plan_hbm.1, s32[4]{0:T(128)} %counts_hbm.1, bf16[432,384]{1,0:T(8,128)(2,1)} %in_w_hbm.1, f32[384]{0:T(512)} %in_b_hbm.1, f32[384]{0:T(512)} %gain_hbm.1, f32[384]{0:T(512)} %nbias_hbm.1, bf16[27,384,384]{2,1,0:T(8,128)(2,1)} %mid_w_hbm.1, ...), custom_call_target="tpu_custom_call" | custom-call | tf_op jit(solution)/shard_map/spans/pallas_call | solution.py:291
  24.2 0.9 %reshape.3 = bf16[1,2,2,61440]{3,2,1,0:T(2,128)(2,1)} reshape(bf16[2,2,160,384]{3,2,1,0:T(8,128)(2,1)S(1)} %spans.1) | data formatting | bytes 983040 | tf_op jit(solution)/shard_map/reshape | solution.py:365
